TPU v7x, 512 devices: a whole 4x8x8 slice. The times are simulated.
512 devices in a mesh: ep: 128 (over z, y, core), tp: 4 (over x).
Axes of the slice: x: 4, y: 8, z: 8, core: 2. Of those that a mesh axis runs over, the one named last changes fastest.
Arguments:
- grad_out: bfloat16 [16384, 3584], P('ep', 'tp'), may hold values from -6 to 6
- routes: int32 [16384, 8], P('ep'), may hold values from 0 to 127, all different within a row; in each aligned block of 128 rows (0 to 127, 128 to 255, ...) at most 10 rows name the same one
- gate_weights: float32 [16384, 8], P('ep'), may hold values from 0.05 to 0.5
- gate_act: bfloat16 [128, 1280, 1024], P('ep', None, 'tp'), may hold values from -6 to 6
- w_down: bfloat16 [128, 1024, 3584], P('ep', None, 'tp'), may hold values from -0.1875 to 0.1875
- w_up: bfloat16 [128, 3584, 1024], P('ep', 'tp'), may hold values from -0.09375 to 0.09375
Outputs:
- grad_in: bfloat16 [16384, 3584], P('ep', 'tp')
Inputs may be any that keep to these rules, and one draw needn't show every extreme that they name: `routes`: each row names 8 different experts; among the 128 rows of one device no expert is named more than 10 times, a bound that some block reaches.
All inputs are finite; a program needn't handle non-finite values.
Results may differ from a plain program's by a relative error of at most 0.02.
Values may be sent and summed in bfloat16 or wider, within the bound.
A program may use at most 64 MiB of HBM per device.

v0:
```python
import jax
import jax.numpy as jnp
from jax import lax
from jax.sharding import PartitionSpec as P


def on_device(grad_out, routes, gate_weights, gate_act, w_down, w_up):
    experts_n = lax.axis_size("ep")
    slot_n = gate_act.shape[1] // experts_n
    rows_n = experts_n * slot_n
    token_n, choose_n = routes.shape
    flat_ids = routes.reshape(-1)
    one_hot = (flat_ids[:, None] == jnp.arange(experts_n, dtype=jnp.int32)[None, :]).astype(
        jnp.int32
    )
    earlier = jnp.cumsum(one_hot, axis=0) - one_hot
    slot_rank = jnp.sum(earlier * one_hot, axis=1)
    position = flat_ids * slot_n + slot_rank
    token_ids = jnp.arange(token_n * choose_n, dtype=jnp.int32) // choose_n
    token_of = jnp.full((rows_n,), token_n, jnp.int32).at[position].set(token_ids)
    weight_of = jnp.zeros((rows_n,), jnp.float32).at[position].set(gate_weights.reshape(-1))
    down_local = w_down[0]
    up_local = w_up[0]
    feat_part = grad_out.shape[1]
    padded = jnp.concatenate([grad_out, jnp.zeros((1, feat_part), grad_out.dtype)], axis=0)
    placed = (padded[token_of].astype(jnp.float32) * weight_of[:, None]).astype(jnp.bfloat16)
    placed = placed.reshape(experts_n, slot_n, feat_part)
    partial_value = jnp.einsum(
        "nsd,fd->nsf",
        lax.all_to_all(placed, "ep", split_axis=0, concat_axis=0, tiled=True),
        down_local,
        preferred_element_type=jnp.float32,
    )
    partial_value = partial_value.reshape(rows_n, -1)
    hidden_grad = lax.psum_scatter(
        partial_value.astype(jnp.bfloat16), "tp", scatter_dimension=1, tiled=True
    ).astype(jnp.float32)
    up_grad = (hidden_grad * gate_act[0].astype(jnp.float32)).astype(jnp.bfloat16)
    row_grad = lax.dot_general(
        lax.all_gather(up_grad, "tp", axis=1, tiled=True),
        up_local,
        (((1,), (1,)), ((), ())),
        preferred_element_type=jnp.float32,
    )
    row_grad = row_grad.astype(jnp.bfloat16).reshape(experts_n, slot_n, -1)
    returned = lax.all_to_all(row_grad, "ep", split_axis=0, concat_axis=0, tiled=True)
    picked = returned.reshape(rows_n, -1)[position]
    summed = jnp.sum(picked.astype(jnp.float32).reshape(token_n, choose_n, -1), axis=1)
    return summed.astype(jnp.bfloat16)


def solution(mesh):
    placed = (
        P("ep", "tp"),
        P("ep", None),
        P("ep", None),
        P("ep", None, "tp"),
        P("ep", None, "tp"),
        P("ep", "tp", None),
    )
    return jax.shard_map(
        on_device, mesh=mesh, in_specs=placed, out_specs=P("ep", "tp"), check_vma=False
    )
```

profile of v0, /device:TPU:24, one launch (start us, length us, event | category | flops | bytes accessed | tf_op | source)
XLA Modules:
  0.0 371.5 jit_solution(9736080060847365617)
XLA Ops:
  6.5 0.8 broadcast_multiply_fusion
  7.4 0.8 copy.8
  8.2 0.1 eq.29
  8.3 0.1 eq.25
  8.4 0.1 copy.7
  8.5 0.1 mul.35
  8.6 0.1 copy.10
  8.7 0.8 copy.12
  9.5 0.1 reshape.105
  9.5 0.2 fusion.5
  9.8 0.1 copy.11
  10.0 0.4 fusion.4
  10.3 4.3 %scatter_custom_fusion = s32[1280]{0:T(1024)S(1)} fusion(s32[1024]{0:T(1024)S(1)} %bitcast.28, s32[1024]{0:T(1024)S(1)} %add_select_fusion, s32[]{:T(128)} %constant.29.clone.1), kind=kCustom, calls=%fused_computation.33 | custom fusion | bytes 5124 | tf_op jit(solution)/shard_map/scatter | solution.py:20
  14.7 4.3 %scatter_custom_fusion.1 = f32[1280]{0:T(1024)S(1)} fusion(s32[1024]{0:T(1024)S(1)} %bitcast.29, f32[1024]{0:T(1024)S(1)} %reshape.105, f32[]{:T(128)} %constant.38.clone.1), kind=kCustom, calls=%fused_computation.31 | custom fusion | bytes 5124 | tf_op jit(solution)/shard_map/scatter | solution.py:21
  19.0 0.1 mul.37
  19.2 5.0 %gather_fusion = bf16[1280,896]{1,0:T(8,128)(2,1)} fusion(bf16[129,896]{1,0:T(8,128)(2,1)S(1)} %concatenate.3, s32[2048]{0:T(1024)S(1)} %pad_clamp_fusion), kind=kCustom, calls=%fused_computation | custom fusion | bytes 4592640 | tf_op jit(solution)/shard_map/gather | solution.py:26
  24.2 5.6 %reshape.75 = f32[128,10,896]{2,1,0:T(8,128)} reshape(bf16[1280,896]{1,0:T(8,128)(2,1)} %gather_fusion) | data formatting | bytes 6881280 | tf_op jit(solution)/shard_map/convert_element_type | solution.py:26
  29.8 3.6 multiply_convert_fusion
  33.4 105.1 %all_to_all.10 = bf16[128,10,896]{2,1,0:T(8,128)(2,1)} all-to-all(bf16[128,10,896]{2,1,0:T(8,128)(2,1)S(1)} %multiply_convert_fusion), channel_id=1, replica_groups=mesh['ep'=128,'tp'=4] {'ep'}, dimensions={0} | all-to-all | bytes 4587520 | tf_op jit(solution)/shard_map/all_to_all | solution.py:30
  138.5 5.3 %dot_general.8 = bf16[1280,896]{1,0:T(8,128)(2,1)} reshape(bf16[128,10,896]{2,1,0:T(8,128)(2,1)} %all_to_all.10) | data formatting | bytes 4587520 | tf_op jit(solution)/shard_map/nsd,fd->nsf/dot_general | solution.py:28
  143.9 5.9 %convolution_convert_fusion = bf16[1280,1024]{1,0:T(8,128)(2,1)} fusion(bf16[1280,896]{1,0:T(8,128)(2,1)} %dot_general.8, bf16[1,1024,896]{2,1,0:T(8,128)(2,1)S(1)} %copy-done), kind=kOutput, calls=%fused_computation.5 | convolution fusion | flops 2350120960 | bytes 6750208 | tf_op jit(solution)/shard_map/nsd,fd->nsf/dot_general | solution.py:28
  149.8 0.0 all-gather.2.cloned.1.call-start
  149.9 37.8 %reduce-scatter.2.cloned.1.call-done = bf16[1280,256]{1,0:T(8,128)(2,1)} async-done(((bf16[1280,1024]{1,0:T(8,128)(2,1)}), bf16[1280,256]{1,0:T(8,128)(2,1)}) %reduce-scatter.2.cloned.1.call-update) | async-done | bytes 655376 | tf_op jit(solution)/shard_map/reduce_scatter | solution.py:35
  187.6 2.1 fusion.2
  189.8 44.1 %all-gather.2.cloned.1.call-done = bf16[1280,1024]{1,0:T(8,128)(2,1)} async-done(((bf16[1280,256]{1,0:T(8,128)(2,1)}), bf16[1280,1024]{1,0:T(8,128)(2,1)}) %all-gather.2.cloned.1.call-update) | async-done | bytes 2621456 | tf_op jit(solution)/shard_map/all_gather | solution.py:40
  233.9 6.7 %convolution_convert_fusion.1 = bf16[1280,896]{1,0:T(8,128)(2,1)} fusion(bf16[1280,1024]{1,0:T(8,128)(2,1)} %all-gather.2.cloned.1.call-done, bf16[1,896,1024]{2,1,0:T(8,128)(2,1)} %param.11), kind=kOutput, calls=%fused_computation.6 | convolution fusion | flops 2349957120 | bytes 6750208 | tf_op jit(solution)/shard_map/dot_general | solution.py:39
  240.5 5.2 %reshape.73 = bf16[128,10,896]{2,1,0:T(8,128)(2,1)} reshape(bf16[1280,896]{1,0:T(8,128)(2,1)} %convolution_convert_fusion.1) | data formatting | bytes 4587520 | tf_op jit(solution)/shard_map/reshape | solution.py:45
  245.7 14.5 %all-to-all-start.1 = ((bf16[128,10,896]{2,1,0:T(8,128)(2,1)}), bf16[128,10,896]{2,1,0:T(8,128)(2,1)}, u32[]{:S(2)}, u32[]{:S(2)}) async-start(bf16[128,10,896]{2,1,0:T(8,128)(2,1)} %reshape.73), calls=%async_computation.2 | async-start | bytes 7340032 | tf_op jit(solution)/shard_map/all_to_all | solution.py:46
  260.2 88.0 %all-to-all-done.1 = bf16[128,10,896]{2,1,0:T(8,128)(2,1)} async-done(((bf16[128,10,896]{2,1,0:T(8,128)(2,1)}), bf16[128,10,896]{2,1,0:T(8,128)(2,1)}, u32[]{:S(2)}, u32[]{:S(2)}) %all-to-all-start.1) | async-done | bytes 2293792 | tf_op jit(solution)/shard_map/all_to_all | solution.py:46
  348.3 5.3 %reshape.74 = bf16[1280,896]{1,0:T(8,128)(2,1)} reshape(bf16[128,10,896]{2,1,0:T(8,128)(2,1)} %all-to-all-done.1) | data formatting | bytes 4587520 | tf_op jit(solution)/shard_map/reshape | solution.py:47
  353.6 7.7 %gather_fusion.1 = bf16[1024,896]{1,0:T(8,128)(2,1)} fusion(bf16[1280,896]{1,0:T(8,128)(2,1)} %reshape.74, s32[1024]{0:T(1024)S(1)} %broadcast_clamp_fusion), kind=kCustom, calls=%fused_computation.1 | custom fusion | bytes 3674112 | tf_op jit(solution)/shard_map/gather | solution.py:47
  361.3 3.4 bitcast_reduce_fusion
  (19 shorter events, 0.2 us)
Async XLA Ops:
  6.5 137.3 %copy-start = (bf16[1,1024,896]{2,1,0:T(8,128)(2,1)S(1)}, bf16[1,1024,896]{2,1,0:T(8,128)(2,1)}, u32[]{:S(2)}) copy-start(bf16[1,1024,896]{2,1,0:T(8,128)(2,1)} %param.10) | copy-start | bytes 5505028
  6.5 12.6 %copy-start.2 = (bf16[128,896]{1,0:T(8,128)(2,1)S(1)}, bf16[128,896]{1,0:T(8,128)(2,1)}, u32[]{:S(2)}) copy-start(bf16[128,896]{1,0:T(8,128)(2,1)} %param.6) | copy-start | bytes 688132
  6.5 181.1 %reduce-scatter.2.cloned.1.call-start = ((), (), s32[]{:S(2)}) async-start(), calls=%async_computation.3 | async-start | bytes 3276800 | tf_op jit(solution)/shard_map/reduce_scatter | solution.py:35
  149.8 37.8 %copy-start.1 = (bf16[1,1280,256]{2,1,0:T(8,128)(2,1)S(1)}, bf16[1,1280,256]{2,1,0:T(8,128)(2,1)}, u32[]{:S(2)}) copy-start(bf16[1,1280,256]{2,1,0:T(8,128)(2,1)} %param.9) | copy-start | bytes 1966084
  149.8 84.0 %all-gather.2.cloned.1.call-start = ((), (), s32[]{:S(2)}) async-start(), calls=%async_computation.4 | async-start | bytes 3276800 | tf_op jit(solution)/shard_map/all_gather | solution.py:40
  245.7 102.6 %all-to-all-start.1 = ((bf16[128,10,896]{2,1,0:T(8,128)(2,1)}), bf16[128,10,896]{2,1,0:T(8,128)(2,1)}, u32[]{:S(2)}, u32[]{:S(2)}) async-start(bf16[128,10,896]{2,1,0:T(8,128)(2,1)} %reshape.73), calls=%async_computation.2 | async-start | bytes 7340032 | tf_op jit(solution)/shard_map/all_to_all | solution.py:46
Sparse Core Ops, SparseCore 0:
  149.9 37.6 reduce-scatter.1
  189.9 43.9 all-gather.1
where the time goes:
time: 372 us
  waiting for transfers between devices  170 us (46%)
  blocking collectives  105 us (28%)
  local copies, waits for them, and re-layouts  45.2 us (12%)
  starting transfers between devices  14.6 us (4%)
  between operations  13.5 us (4%)
  matrix products  12.6 us (3%)
  other arithmetic  10.6 us (3%)
    all_to_all x1, blocking collectives, on_device(): lax.all_to_all(placed, 'ep', split_axis=0, concat_axis=0, tiled=True)  105 us
    all_to_all x1, waiting for transfers between devices, on_device(): lax.all_to_all(row_grad, 'ep', split_axis=0, concat_axis=0, tiled=True)  88 us
    all_gather x1, waiting for transfers between devices, on_device(): lax.all_gather(up_grad, 'tp', axis=1, tiled=True)  44.1 us
    reduce_scatter x1, waiting for transfers between devices, on_device(): lax.psum_scatter(partial_value.astype(jnp.bfloat16), 'tp', scatter_dimens...  37.8 us
    all_to_all x1, starting transfers between devices, on_device(): lax.all_to_all(row_grad, 'ep', split_axis=0, concat_axis=0, tiled=True)  14.5 us
    gather x1, local copies, waits for them, and re-layouts, on_device(): picked = returned.reshape(rows_n, -1)[position]  7.67 us
  transfers between devices with their start and end apart: 3, of which 3 were waited for; matrix products, arithmetic and copies ran while one was open for 0% of the time, Pallas kernels for 0%

commit v1 on v0

--- a/solution.py
+++ b/solution.py
@@ -37,7 +37,9 @@
     ).astype(jnp.float32)
     up_grad = (hidden_grad * gate_act[0].astype(jnp.float32)).astype(jnp.bfloat16)
     row_grad = lax.dot_general(
-        lax.all_gather(up_grad, "tp", axis=1, tiled=True),
+        jnp.concatenate(
+            lax.all_to_all(jnp.stack([up_grad] * lax.axis_size("tp")), "tp", 0, 0), axis=1
+        ),
         up_local,
         (((1,), (1,)), ((), ())),
         preferred_element_type=jnp.float32,

time: 372 us -> 360 us (0.968)
  waiting for transfers between devices: 170 us -> 126 us
  blocking collectives: 105 us -> 140 us
    all_gather x1 -> x0, waiting for transfers between devices: 44.1 us -> none  [on_device(): lax.all_gather(up_grad, 'tp', axis=1, tiled=True)]
    all_to_all x0 -> x1, blocking collectives: none -> 34.9 us  [on_device(): lax.all_to_all(jnp.stack([up_grad] * lax.axis_size('tp')), 'tp', 0, 0)]
  transfers between devices with their start and end apart: 3 -> 2, of which waited for: 3 -> 2; matrix products, arithmetic and copies ran while one was open for 0% -> 0% of each run, Pallas kernels for 0% -> 0%
where the time goes in v1:
time: 360 us; the launch traced here: 359 us
  blocking collectives  140 us (39%)
  waiting for transfers between devices  126 us (35%)
  local copies, waits for them, and re-layouts  45.6 us (13%)
  starting transfers between devices  14.5 us (4%)
  between operations  13.5 us (4%)
  matrix products  10.2 us (3%)
  other arithmetic  9.74 us (3%)
    all_to_all x1, blocking collectives, on_device(): lax.all_to_all(placed, 'ep', split_axis=0, concat_axis=0, tiled=True)  105 us
    all_to_all x1, waiting for transfers between devices, on_device(): lax.all_to_all(row_grad, 'ep', split_axis=0, concat_axis=0, tiled=True)  88 us
    reduce_scatter x1, waiting for transfers between devices, on_device(): lax.psum_scatter(partial_value.astype(jnp.bfloat16), 'tp', scatter_dimens...  37.8 us
    all_to_all x1, blocking collectives, on_device(): lax.all_to_all(jnp.stack([up_grad] * lax.axis_size('tp')), 'tp', 0, 0)  34.9 us
    all_to_all x1, starting transfers between devices, on_device(): lax.all_to_all(row_grad, 'ep', split_axis=0, concat_axis=0, tiled=True)  14.5 us
    gather x1, local copies, waits for them, and re-layouts, on_device(): picked = returned.reshape(rows_n, -1)[position]  7.67 us
  transfers between devices with their start and end apart: 2, of which 2 were waited for; matrix products, arithmetic and copies ran while one was open for 0% of the time, Pallas kernels for 0%

profile of v1, /device:TPU:24, one launch (start us, length us, event | category | flops | bytes accessed | tf_op | source)
XLA Modules:
  0.0 359.4 jit_solution(16583294730819005968)
XLA Ops:
  6.5 0.8 broadcast_multiply_fusion
  7.4 0.8 copy.8
  8.2 0.1 eq.29
  8.4 0.1 copy.7
  8.5 0.1 mul.35
  8.6 0.1 copy.10
  8.7 0.8 copy.12
  9.5 0.1 reshape.115
  9.5 0.2 fusion.5
  9.8 0.1 copy.11
  10.0 0.4 fusion.4
  10.3 4.3 %scatter_custom_fusion = s32[1280]{0:T(1024)S(1)} fusion(s32[1024]{0:T(1024)S(1)} %bitcast.32, s32[1024]{0:T(1024)S(1)} %add_select_fusion, s32[]{:T(128)} %constant.29.clone.1), kind=kCustom, calls=%fused_computation.33 | custom fusion | bytes 5124 | tf_op jit(solution)/shard_map/scatter | solution.py:20
  14.7 4.3 %scatter_custom_fusion.1 = f32[1280]{0:T(1024)S(1)} fusion(s32[1024]{0:T(1024)S(1)} %bitcast.33, f32[1024]{0:T(1024)S(1)} %reshape.115, f32[]{:T(128)} %constant.38.clone.1), kind=kCustom, calls=%fused_computation.31 | custom fusion | bytes 5124 | tf_op jit(solution)/shard_map/scatter | solution.py:21
  19.0 0.1 mul.37
  19.2 5.0 %gather_fusion = bf16[1280,896]{1,0:T(8,128)(2,1)} fusion(bf16[129,896]{1,0:T(8,128)(2,1)S(1)} %concatenate.3, s32[2048]{0:T(1024)S(1)} %pad_clamp_fusion), kind=kCustom, calls=%fused_computation | custom fusion | bytes 4592640 | tf_op jit(solution)/shard_map/gather | solution.py:26
  24.2 5.6 %reshape.85 = f32[128,10,896]{2,1,0:T(8,128)} reshape(bf16[1280,896]{1,0:T(8,128)(2,1)} %gather_fusion) | data formatting | bytes 6881280 | tf_op jit(solution)/shard_map/convert_element_type | solution.py:26
  29.8 3.6 multiply_convert_fusion
  33.4 105.1 %all_to_all.15 = bf16[128,10,896]{2,1,0:T(8,128)(2,1)} all-to-all(bf16[128,10,896]{2,1,0:T(8,128)(2,1)S(1)} %multiply_convert_fusion), channel_id=1, replica_groups=mesh['ep'=128,'tp'=4] {'ep'}, dimensions={0} | all-to-all | bytes 4587520 | tf_op jit(solution)/shard_map/all_to_all | solution.py:30
  138.5 5.3 %dot_general.8 = bf16[1280,896]{1,0:T(8,128)(2,1)} reshape(bf16[128,10,896]{2,1,0:T(8,128)(2,1)} %all_to_all.15) | data formatting | bytes 4587520 | tf_op jit(solution)/shard_map/nsd,fd->nsf/dot_general | solution.py:28
  143.9 5.9 %convolution_convert_fusion = bf16[1280,1024]{1,0:T(8,128)(2,1)} fusion(bf16[1280,896]{1,0:T(8,128)(2,1)} %dot_general.8, bf16[1,1024,896]{2,1,0:T(8,128)(2,1)S(1)} %copy-done), kind=kOutput, calls=%fused_computation.5 | convolution fusion | flops 2350120960 | bytes 6750208 | tf_op jit(solution)/shard_map/nsd,fd->nsf/dot_general | solution.py:28
  149.8 37.8 %reduce-scatter.2.cloned.1.call-done = bf16[1280,256]{1,0:T(8,128)(2,1)} async-done(((bf16[1280,1024]{1,0:T(8,128)(2,1)}), bf16[1280,256]{1,0:T(8,128)(2,1)}) %reduce-scatter.2.cloned.1.call-update) | async-done | bytes 655376 | tf_op jit(solution)/shard_map/reduce_scatter | solution.py:35
  187.6 1.3 fusion.2
  188.9 0.2 copy.13
  189.1 0.2 stack.2
  189.3 34.9 %all_to_all.16 = bf16[4,1280,256]{1,2,0:T(8,128)(2,1)S(1)} all-to-all(bf16[4,1280,256]{1,2,0:T(8,128)(2,1)S(1)} %stack.2), channel_id=1, replica_groups=mesh['ep'=128,'tp'=4] {'tp'}, dimensions={0} | all-to-all | bytes 5242880 | tf_op jit(solution)/shard_map/all_to_all | solution.py:41
  224.2 4.2 %convolution_convert_fusion.1 = bf16[1280,896]{1,0:T(8,128)(2,1)} fusion(bf16[1280,1024]{0,1:T(8,128)(2,1)S(1)} %bitcast.30, bf16[1,896,1024]{2,1,0:T(8,128)(2,1)S(1)} %copy-done.3), kind=kOutput, calls=%fused_computation.6 | convolution fusion | flops 2349957120 | bytes 6750208 | tf_op jit(solution)/shard_map/dot_general | solution.py:39
  228.4 5.2 %reshape.83 = bf16[128,10,896]{2,1,0:T(8,128)(2,1)} reshape(bf16[1280,896]{1,0:T(8,128)(2,1)} %convolution_convert_fusion.1) | data formatting | bytes 4587520 | tf_op jit(solution)/shard_map/reshape | solution.py:47
  233.6 14.5 %all-to-all-start.2 = ((bf16[128,10,896]{2,1,0:T(8,128)(2,1)}), bf16[128,10,896]{2,1,0:T(8,128)(2,1)}, u32[]{:S(2)}, u32[]{:S(2)}) async-start(bf16[128,10,896]{2,1,0:T(8,128)(2,1)} %reshape.83), calls=%async_computation.3 | async-start | bytes 7340032 | tf_op jit(solution)/shard_map/all_to_all | solution.py:48
  248.1 88.0 %all-to-all-done.2 = bf16[128,10,896]{2,1,0:T(8,128)(2,1)} async-done(((bf16[128,10,896]{2,1,0:T(8,128)(2,1)}), bf16[128,10,896]{2,1,0:T(8,128)(2,1)}, u32[]{:S(2)}, u32[]{:S(2)}) %all-to-all-start.2) | async-done | bytes 2293792 | tf_op jit(solution)/shard_map/all_to_all | solution.py:48
  336.2 5.3 %reshape.84 = bf16[1280,896]{1,0:T(8,128)(2,1)} reshape(bf16[128,10,896]{2,1,0:T(8,128)(2,1)} %all-to-all-done.2) | data formatting | bytes 4587520 | tf_op jit(solution)/shard_map/reshape | solution.py:49
  341.5 7.7 %gather_fusion.1 = bf16[1024,896]{1,0:T(8,128)(2,1)} fusion(bf16[1280,896]{1,0:T(8,128)(2,1)} %reshape.84, s32[1024]{0:T(1024)S(1)} %broadcast_clamp_fusion), kind=kCustom, calls=%fused_computation.1 | custom fusion | bytes 3674112 | tf_op jit(solution)/shard_map/gather | solution.py:49
  349.2 3.4 bitcast_reduce_fusion
  (21 shorter events, 0.2 us)
Async XLA Ops:
  6.5 137.3 %copy-start = (bf16[1,1024,896]{2,1,0:T(8,128)(2,1)S(1)}, bf16[1,1024,896]{2,1,0:T(8,128)(2,1)}, u32[]{:S(2)}) copy-start(bf16[1,1024,896]{2,1,0:T(8,128)(2,1)} %param.10) | copy-start | bytes 5505028
  6.5 12.6 %copy-start.2 = (bf16[128,896]{1,0:T(8,128)(2,1)S(1)}, bf16[128,896]{1,0:T(8,128)(2,1)}, u32[]{:S(2)}) copy-start(bf16[128,896]{1,0:T(8,128)(2,1)} %param.6) | copy-start | bytes 688132
  6.5 181.1 %reduce-scatter.2.cloned.1.call-start = ((), (), s32[]{:S(2)}) async-start(), calls=%async_computation.4 | async-start | bytes 3276800 | tf_op jit(solution)/shard_map/reduce_scatter | solution.py:35
  149.8 37.8 %copy-start.1 = (bf16[1,1280,256]{2,1,0:T(8,128)(2,1)S(1)}, bf16[1,1280,256]{2,1,0:T(8,128)(2,1)}, u32[]{:S(2)}) copy-start(bf16[1,1280,256]{2,1,0:T(8,128)(2,1)} %param.9) | copy-start | bytes 1966084
  189.3 34.9 %copy-start.3 = (bf16[1,896,1024]{2,1,0:T(8,128)(2,1)S(1)}, bf16[1,896,1024]{2,1,0:T(8,128)(2,1)}, u32[]{:S(2)}) copy-start(bf16[1,896,1024]{2,1,0:T(8,128)(2,1)} %param.11) | copy-start | bytes 5505028
  233.6 102.5 %all-to-all-start.2 = ((bf16[128,10,896]{2,1,0:T(8,128)(2,1)}), bf16[128,10,896]{2,1,0:T(8,128)(2,1)}, u32[]{:S(2)}, u32[]{:S(2)}) async-start(bf16[128,10,896]{2,1,0:T(8,128)(2,1)} %reshape.83), calls=%async_computation.3 | async-start | bytes 7340032 | tf_op jit(solution)/shard_map/all_to_all | solution.py:48
Sparse Core Ops, SparseCore 0:
  149.9 37.6 reduce-scatter.1
